TPU v7x, 256 devices: a whole 4x4x8 slice. The times are simulated.
256 devices in a mesh: freq: 128 (over z, y_lo, x, core), col: 2 (over y_hi).
Axes of the slice: x: 4, y: 4 (y_hi: 2, y_lo: 2; y = y_hi * 2 + y_lo), z: 8, core: 2. Of those that a mesh axis runs over, the one named last changes fastest.
Arguments:
- traces: bfloat16 [1024, 1024, 1024], P('freq', 'col'), may hold values from -6 to 6
- source_row: int32 [1024], replicated, may hold values from 0 to 1023, each once
Outputs:
- multiples: bfloat16 [2, 128, 1024, 1024], P(None, 'freq', None, 'col')
Inputs may be any that keep to these rules, and one draw needn't show every extreme that they name: `source_row`: a permutation of the 1024 acquisition rows.
All inputs are finite; a program needn't handle non-finite values.
Results may differ from a plain program's by a relative error of at most 0.0079.
Values may be sent and summed in bfloat16 or wider, within the bound.
No kernel may reach another device: no remote copies, remote signals or barrier semaphores. Data moves between devices by JAX's collectives and lax.ppermute only.
A program may use at most 64 MiB of HBM per device.

v0:
```python
import math
import jax
import jax.numpy as jnp
from jax import lax
from jax.sharding import PartitionSpec as P


def partner(value, axis, bit):
    return lax.ppermute(value, axis, [(i, i ^ 1 << bit) for i in range(lax.axis_size(axis))])


def dft_table(samples, kept):
    row_index = jnp.arange(2 * kept)
    frequency = (row_index % kept)[:, None]
    sample_index = jnp.arange(samples)[None, :]
    phase = frequency * sample_index % samples
    angle = 2.0 * math.pi / samples * phase.astype(jnp.float32)
    table = jnp.where(row_index[:, None] < kept, jnp.cos(angle), -jnp.sin(angle))
    return (table / jnp.sqrt(jnp.float32(samples))).astype(jnp.bfloat16)


def single_product(first, second):
    return jnp.einsum("fnk,fkh->fnh", first, second, preferred_element_type=jnp.float32)


def complex_product(left, right):
    real_part = single_product(left[0], right[0]) - single_product(left[1], right[1])
    imag_part = single_product(left[0], right[1]) + single_product(left[1], right[0])
    return jnp.stack([real_part, imag_part])


def ordered(own_block, other_block, is_first, concat_axis):
    upper = jnp.where(is_first, own_block, other_block)
    lower = jnp.where(is_first, other_block, own_block)
    return jnp.concatenate([upper, lower], concat_axis)


def mirror(block):
    return jnp.swapaxes(block, 2, 3)


def average(first, second):
    return ((first.astype(jnp.float32) + second.astype(jnp.float32)) * 0.5).astype(jnp.bfloat16)


def shards(traces, source_row):
    samples = traces.shape[2]
    kept = samples // 8
    table = dft_table(samples, kept)
    spectrum = jnp.einsum("kt,srt->ksr", table, traces, preferred_element_type=jnp.float32).astype(
        jnp.bfloat16
    )
    spectrum = spectrum.reshape(2, kept, traces.shape[0], traces.shape[1])
    acquired = lax.all_to_all(spectrum, "freq", split_axis=1, concat_axis=2, tiled=True)
    arranged = jnp.take(acquired, source_row, axis=2)
    width = arranged.shape[3]
    column_half = lax.axis_index("col")
    is_first = column_half == 0
    mine = lax.dynamic_slice_in_dim(arranged, column_half * width, width, 2)
    theirs = lax.dynamic_slice_in_dim(arranged, (1 - column_half) * width, width, 2)
    mirrored = partner(theirs, "col", 0)
    transposed = ordered(mirror(mine), mirror(mirrored), is_first, 2)
    spectral = average(arranged, transposed)
    whole = lax.all_gather(spectral, "col", axis=3, tiled=True)
    scale = 1.0 / math.sqrt(spectral.shape[2])
    square = (scale * complex_product(whole, spectral)).astype(jnp.bfloat16)
    cube = scale * complex_product(whole, square)
    return (spectral.astype(jnp.float32) - square.astype(jnp.float32) + cube).astype(jnp.bfloat16)


def solution(mesh):
    in_specs = (P("freq", "col", None), P())
    out_specs = P(None, "freq", None, "col")
    return jax.shard_map(shards, mesh=mesh, in_specs=in_specs, out_specs=out_specs, check_vma=False)
```

profile of v0, /device:TPU:1, one launch (start us, length us, event | category | flops | bytes accessed | tf_op | source)
XLA Modules:
  0.0 218.2 jit_solution(4405129899482517952)
XLA Ops:
  6.5 9.8 %convolution_convert_fusion = bf16[256,8,512]{2,0,1:T(8,128)(2,1)S(1)} fusion(bf16[8,512,1024]{2,1,0:T(8,128)(2,1)} %param.2, s32[256]{0:T(256)S(1)} %and_select_fusion, pred[256]{0:T(512)(128)(4,1)S(1)} %iota_compare_fusion), kind=kOutput, calls=%fused_computation.15 | convolution fusion | flops 2153250816 | bytes 10487040 | tf_op jit(solution)/shard_map/kt,srt->ksr/dot_general | solution.py:50
  16.4 2.5 %copy.8 = bf16[2,128,8,512]{3,2,0,1:T(8,128)(2,1)} copy(bf16[2,128,8,512]{3,1,0,2:T(8,128)(2,1)S(1)} %bitcast.53) | data formatting | bytes 4194304 | tf_op jit(solution)/shard_map/reshape | solution.py:53
  18.9 0.0 copy-start.2
  18.9 14.9 %all-to-all-start = ((bf16[2,128,8,512]{3,2,0,1:T(8,128)(2,1)}), bf16[2,128,8,512]{3,2,0,1:T(8,128)(2,1)S(1)}, u32[]{:S(2)}, u32[]{:S(2)}) async-start(bf16[2,128,8,512]{3,2,0,1:T(8,128)(2,1)} %copy.8), calls=%async_computation | async-start | bytes 4194304 | tf_op jit(solution)/shard_map/all_to_all | solution.py:54
  33.8 0.2 all-gather.2.cloned.1.call-start
  34.0 0.0 copy-done.2
  34.1 50.9 %all-to-all-done = bf16[2,128,8,512]{3,2,0,1:T(8,128)(2,1)S(1)} async-done(((bf16[2,128,8,512]{3,2,0,1:T(8,128)(2,1)}), bf16[2,128,8,512]{3,2,0,1:T(8,128)(2,1)S(1)}, u32[]{:S(2)}, u32[]{:S(2)}) %all-to-all-start) | async-done | bytes 2097184 | tf_op jit(solution)/shard_map/all_to_all | solution.py:54
  85.0 0.2 copy.14
  85.1 2.2 copy.10
  87.3 10.9 %gather_fusion = bf16[1024,2,512]{2,1,0:T(2,128)(2,1)} fusion(bf16[2,1024,512]{2,0,1:T(2,128)(2,1)S(1)} %copy.10, s32[1024]{0:T(1024)S(1)} %fusion.22), kind=kCustom, calls=%fused_computation | custom fusion | bytes 4198400 | tf_op jit(solution)/shard_map/jit(_take)/gather | solution.py:55
  98.2 6.2 %copy.11 = bf16[1024,2,512]{0,2,1:T(8,128)(2,1)} copy(bf16[1024,2,512]{2,1,0:T(2,128)(2,1)} %gather_fusion) | data formatting | bytes 4194304 | tf_op jit(solution)/shard_map/jit(_take)/gather | solution.py:55
  104.5 1.8 bitcast_select_fusion
  106.3 1.1 constant_dynamic-slice_fusion
  107.3 2.6 %collective-permute-start = (bf16[2,1,512,512]{2,3,1,0:T(8,128)(2,1)}, bf16[2,1,512,512]{2,3,1,0:T(8,128)(2,1)S(1)}, u32[]{:S(2)}, u32[]{:S(2)}) collective-permute-start(bf16[2,1,512,512]{2,3,1,0:T(8,128)(2,1)} %constant_dynamic-slice_fusion), channel_id=1, source_target_pairs={{0,1},{1,0},{2,3},{3,2},{4,5},{5,4},{6,7},{7,6},{8,9},{9,8},{10,11... | collective-permute-start | bytes 3145736 | tf_op jit(solution)/shard_map/ppermute | solution.py:9
  110.0 3.0 %copy.12 = f32[2,1,1024,512]{3,2,1,0:T(8,128)} copy(bf16[2,1,1024,512]{2,3,1,0:T(8,128)(2,1)S(1)} %bitcast_select_fusion) | data formatting | bytes 6291456 | tf_op jit(solution)/shard_map/convert_element_type | solution.py:43
  112.9 0.0 copy-start.1
  112.9 20.4 %collective-permute-done = bf16[2,1,512,512]{2,3,1,0:T(8,128)(2,1)S(1)} collective-permute-done((bf16[2,1,512,512]{2,3,1,0:T(8,128)(2,1)}, bf16[2,1,512,512]{2,3,1,0:T(8,128)(2,1)S(1)}, u32[]{:S(2)}, u32[]{:S(2)}) %collective-permute-start) | collective-permute-done | bytes 1048608 | tf_op jit(solution)/shard_map/ppermute | solution.py:9
  133.4 0.5 select_bitcast_fusion.1
  133.8 0.0 copy-done.1
  133.9 2.1 multiply_convert_fusion
  136.0 0.0 copy-start
  136.0 0.0 all-gather.2.cloned.1.call-update
  136.0 60.8 %all-gather.2.cloned.1.call-done = bf16[2,1,1024,1024]{3,2,1,0:T(8,128)(2,1)} async-done(((bf16[2,1,1024,512]{3,2,1,0:T(8,128)(2,1)}), bf16[2,1,1024,1024]{3,2,1,0:T(8,128)(2,1)}) %all-gather.2.cloned.1.call-update) | async-done | bytes 4194320 | tf_op jit(solution)/shard_map/all_gather | solution.py:64
  196.7 0.0 copy-done
  196.7 0.0 copy-start.3
  196.7 3.0 %fusion.5 = f32[1024,512]{1,0:T(8,128)S(1)} fusion(bf16[2,1,1024,1024]{3,2,1,0:T(8,128)(2,1)} %all-gather.2.cloned.1.call-done, bf16[2,1,1024,512]{3,2,1,0:T(8,128)(2,1)S(1)} %copy-done), kind=kOutput, calls=%fused_computation.21 | convolution fusion | flops 1073741824 | bytes 5242880 | tf_op jit(solution)/shard_map/fnk,fkh->fnh/dot_general | solution.py:23
  199.7 0.0 copy-done.3
  199.7 1.2 fusion.6
  201.0 1.2 add_bitcast_fusion.1
  202.2 1.2 subtract_bitcast_fusion.1
  203.5 0.6 fusion
  204.1 1.2 fusion.4
  205.3 1.2 fusion.3
  206.6 1.2 subtract_bitcast_fusion
  207.8 1.3 add_bitcast_fusion
  209.1 2.3 %fusion.2 = bf16[2,1,1024,512]{3,2,1,0:T(8,128)(2,1)} fusion(f32[1,1,1024,512]{3,2,1,0:T(8,128)S(1)} %add_bitcast_fusion, f32[1,1,1024,512]{3,2,1,0:T(8,128)S(1)} %subtract_bitcast_fusion, bf16[2,1,1024,512]{3,2,1,0:T(8,128)(2,1)S(1)} %copy-done, f32[1,1,1024,512]{3,2,1,0:T(8,128)S(1)} %add_bitcast_fusion.1, f32[1,1,1024,512]{3,2,1,0:T(8,128)S(1)} %subtract_bitcast_fusion.1), kind=kLoop, calls=%fused_computation.5 | loop fusion | flops 10485760 | bytes 12582912 | tf_op jit(solution)/shard_map/convert_element_type | solution.py:68
  (4 shorter events, 0.0 us)
Async XLA Ops:
  18.9 15.1 %copy-start.2 = (s32[1024]{0:T(1024)S(1)}, s32[1024]{0:T(1024)}, u32[]{:S(2)}) copy-start(s32[1024]{0:T(1024)} %param.3) | copy-start | bytes 12292
  18.9 66.1 %all-to-all-start = ((bf16[2,128,8,512]{3,2,0,1:T(8,128)(2,1)}), bf16[2,128,8,512]{3,2,0,1:T(8,128)(2,1)S(1)}, u32[]{:S(2)}, u32[]{:S(2)}) async-start(bf16[2,128,8,512]{3,2,0,1:T(8,128)(2,1)} %copy.8), calls=%async_computation | async-start | bytes 4194304 | tf_op jit(solution)/shard_map/all_to_all | solution.py:54
  33.8 163.0 %all-gather.2.cloned.1.call-start = ((), (), s32[]{:S(2)}) async-start(), calls=%async_computation.1 | async-start | bytes 6291456 | tf_op jit(solution)/shard_map/all_gather | solution.py:64
  107.3 26.0 %collective-permute-start = (bf16[2,1,512,512]{2,3,1,0:T(8,128)(2,1)}, bf16[2,1,512,512]{2,3,1,0:T(8,128)(2,1)S(1)}, u32[]{:S(2)}, u32[]{:S(2)}) collective-permute-start(bf16[2,1,512,512]{2,3,1,0:T(8,128)(2,1)} %constant_dynamic-slice_fusion), channel_id=1, source_target_pairs={{0,1},{1,0},{2,3},{3,2},{4,5},{5,4},{6,7},{7,6},{8,9},{9,8},{10,11... | collective-permute-start | bytes 3145736 | tf_op jit(solution)/shard_map/ppermute | solution.py:9
  112.9 20.9 %copy-start.1 = (f32[2,1,1024,512]{3,2,1,0:T(8,128)S(1)}, f32[2,1,1024,512]{3,2,1,0:T(8,128)}, u32[]{:S(2)}) copy-start(f32[2,1,1024,512]{3,2,1,0:T(8,128)} %copy.12) | copy-start | bytes 12582916
  136.0 60.8 %copy-start = (bf16[2,1,1024,512]{3,2,1,0:T(8,128)(2,1)S(1)}, bf16[2,1,1024,512]{3,2,1,0:T(8,128)(2,1)}, u32[]{:S(2)}) copy-start(bf16[2,1,1024,512]{3,2,1,0:T(8,128)(2,1)} %multiply_convert_fusion) | copy-start | bytes 6291460
  196.7 3.0 %copy-start.3 = (bf16[2,1,1024,1024]{3,2,1,0:T(8,128)(2,1)S(1)}, bf16[2,1,1024,1024]{3,2,1,0:T(8,128)(2,1)}, u32[]{:S(2)}) copy-start(bf16[2,1,1024,1024]{3,2,1,0:T(8,128)(2,1)} %all-gather.2.cloned.1.call-done) | copy-start | bytes 12582916
Sparse Core Ops, SparseCore 0:
  136.1 60.5 all-gather.1
where the time goes:
time: 219 us; the launch traced here: 218 us
  waiting for transfers between devices  132 us (60%)
  local copies, waits for them, and re-layouts  26 us (12%)
  matrix products  21.5 us (10%)
  starting transfers between devices  17.7 us (8%)
  between operations  13.5 us (6%)
  other arithmetic  7.23 us (3%)
    all_gather x1, waiting for transfers between devices, shards(): whole = lax.all_gather(spectral, 'col', axis=3, tiled=True)  60.8 us
    all_to_all x1, waiting for transfers between devices, shards(): lax.all_to_all(spectrum, 'freq', split_axis=1, concat_axis=2, tiled=True)  50.9 us
    ppermute x1, waiting for transfers between devices, partner(): lax.ppermute(value, axis, [(i, i ^ 1 << bit) for i in range(lax.axis_size...  20.4 us
    gather x2, local copies, waits for them, and re-layouts, shards(): arranged = jnp.take(acquired, source_row, axis=2)  17.1 us
    all_to_all x1, starting transfers between devices, shards(): lax.all_to_all(spectrum, 'freq', split_axis=1, concat_axis=2, tiled=True)  14.9 us
    dot_general x8, matrix products, single_product(): jnp.einsum('fnk,fkh->fnh', first, second, preferred_element_type=jnp.floa...  11.7 us
    dot_general x1, matrix products, shards(): jnp.einsum('kt,srt->ksr', table, traces, preferred_element_type=jnp.float32)  9.83 us
  transfers between devices with their start and end apart: 3, of which 3 were waited for; matrix products, arithmetic and copies ran while one was open for 1% of the time, Pallas kernels for 0%

commit v1 on v0

--- a/solution.py
+++ b/solution.py
@@ -51,7 +51,10 @@
         jnp.bfloat16
     )
     spectrum = spectrum.reshape(2, kept, traces.shape[0], traces.shape[1])
-    acquired = lax.all_to_all(spectrum, "freq", split_axis=1, concat_axis=2, tiled=True)
+    acquired = jnp.concatenate(
+        lax.all_to_all(jnp.stack(jnp.split(spectrum, lax.axis_size("freq"), axis=1)), "freq", 0, 0),
+        axis=2,
+    )
     arranged = jnp.take(acquired, source_row, axis=2)
     width = arranged.shape[3]
     column_half = lax.axis_index("col")

time: 219 us -> 302 us (1.38)
  local copies, waits for them, and re-layouts: 26 us -> 109 us
    unnamed x8 -> x137, local copies, waits for them, and re-layouts: 0.01 us -> 79.2 us
    split x0 -> x7, local copies, waits for them, and re-layouts: none -> 4.45 us  [shards(): jnp.split(spectrum, lax.axis_size('freq'), axis=1)]
where the time goes in v1:
time: 302 us
  waiting for transfers between devices  132 us (44%)
  local copies, waits for them, and re-layouts  109 us (36%)
  matrix products  21.5 us (7%)
  starting transfers between devices  17.6 us (6%)
  between operations  13.7 us (5%)
  other arithmetic  7.23 us (2%)
    unnamed x137, local copies, waits for them, and re-layouts  79.2 us
    all_gather x1, waiting for transfers between devices, shards(): whole = lax.all_gather(spectral, 'col', axis=3, tiled=True)  60.8 us
    all_to_all x1, waiting for transfers between devices, shards(): lax.all_to_all(jnp.stack(jnp.split(spectrum, lax.axis_size('freq'), axis=...  51.1 us
    ppermute x1, waiting for transfers between devices, partner(): lax.ppermute(value, axis, [(i, i ^ 1 << bit) for i in range(lax.axis_size...  20.4 us
    gather x2, local copies, waits for them, and re-layouts, shards(): arranged = jnp.take(acquired, source_row, axis=2)  17.1 us
    all_to_all x1, starting transfers between devices, shards(): lax.all_to_all(jnp.stack(jnp.split(spectrum, lax.axis_size('freq'), axis=...  14.9 us
    dot_general x8, matrix products, single_product(): jnp.einsum('fnk,fkh->fnh', first, second, preferred_element_type=jnp.floa...  11.7 us
    dot_general x1, matrix products, shards(): jnp.einsum('kt,srt->ksr', table, traces, preferred_element_type=jnp.float32)  9.83 us
  transfers between devices with their start and end apart: 3, of which 3 were waited for; matrix products, arithmetic and copies ran while one was open for 1% of the time, Pallas kernels for 0%

profile of v1, /device:TPU:1, one launch (start us, length us, event | category | flops | bytes accessed | tf_op | source)
XLA Modules:
  0.0 301.7 jit_solution(18191914180686490493)
XLA Ops:
  6.5 9.8 %convolution_convert_fusion = bf16[256,8,512]{2,0,1:T(8,128)(2,1)S(1)} fusion(bf16[8,512,1024]{2,1,0:T(8,128)(2,1)} %param.2, s32[256]{0:T(256)S(1)} %and_select_fusion, pred[256]{0:T(512)(128)(4,1)S(1)} %iota_compare_fusion), kind=kOutput, calls=%fused_computation.14 | convolution fusion | flops 2153250816 | bytes 10487040 | tf_op jit(solution)/shard_map/kt,srt->ksr/dot_general | solution.py:50
  16.9 0.6 fusion.33
  17.5 0.7 fusion.31
  18.2 0.7 fusion.32
  18.9 0.7 fusion.29
  19.6 0.6 fusion.30
  20.2 0.7 fusion.28
  20.9 0.6 constant_dynamic-update-slice_fusion.127
  21.5 0.6 constant_dynamic-update-slice_fusion.126
  22.1 0.6 constant_dynamic-update-slice_fusion.125
  22.7 0.6 constant_dynamic-update-slice_fusion.124
  23.3 0.6 constant_dynamic-update-slice_fusion.123
  24.0 0.6 constant_dynamic-update-slice_fusion.122
  24.6 0.6 constant_dynamic-update-slice_fusion.121
  25.2 0.6 constant_dynamic-update-slice_fusion.120
  26.4 0.6 constant_dynamic-update-slice_fusion.118
  27.0 0.6 constant_dynamic-update-slice_fusion.117
  27.6 0.6 constant_dynamic-update-slice_fusion.116
  28.3 0.6 constant_dynamic-update-slice_fusion.115
  29.5 0.6 constant_dynamic-update-slice_fusion.113
  30.1 0.6 constant_dynamic-update-slice_fusion.112
  30.7 0.6 constant_dynamic-update-slice_fusion.111
  31.3 0.6 constant_dynamic-update-slice_fusion.110
  31.9 0.6 constant_dynamic-update-slice_fusion.109
  32.6 0.6 constant_dynamic-update-slice_fusion.108
  33.2 0.6 constant_dynamic-update-slice_fusion.107
  33.8 0.6 constant_dynamic-update-slice_fusion.106
  34.4 0.6 constant_dynamic-update-slice_fusion.105
  35.0 0.6 constant_dynamic-update-slice_fusion.104
  35.6 0.6 constant_dynamic-update-slice_fusion.103
  36.2 0.6 constant_dynamic-update-slice_fusion.102
  36.9 0.6 constant_dynamic-update-slice_fusion.101
  38.1 0.6 constant_dynamic-update-slice_fusion.99
  38.7 0.6 constant_dynamic-update-slice_fusion.98
  39.3 0.6 constant_dynamic-update-slice_fusion.97
  39.9 0.6 constant_dynamic-update-slice_fusion.96
  41.1 0.6 constant_dynamic-update-slice_fusion.94
  41.8 0.6 constant_dynamic-update-slice_fusion.93
  42.4 0.6 constant_dynamic-update-slice_fusion.92
  43.0 0.6 constant_dynamic-update-slice_fusion.91
  43.6 0.6 constant_dynamic-update-slice_fusion.90
  92.1 0.6 constant_dynamic-update-slice_fusion.11
  99.4 14.9 %all-to-all-start = ((bf16[128,2,1,8,512]{4,3,1,2,0:T(8,128)(2,1)}), bf16[128,2,1,8,512]{4,3,1,2,0:T(8,128)(2,1)S(1)}, u32[]{:S(2)}, u32[]{:S(2)}) async-start(bf16[128,2,1,8,512]{4,3,1,2,0:T(8,128)(2,1)} %constant_dynamic-update-slice_fusion), calls=%async_computation | async-start | bytes 4194304 | tf_op jit(solution)/shard_map/all_to_all | solution.py:55
  114.4 51.1 %all-to-all-done = bf16[128,2,1,8,512]{4,3,1,2,0:T(8,128)(2,1)S(1)} async-done(((bf16[128,2,1,8,512]{4,3,1,2,0:T(8,128)(2,1)}), bf16[128,2,1,8,512]{4,3,1,2,0:T(8,128)(2,1)S(1)}, u32[]{:S(2)}, u32[]{:S(2)}) %all-to-all-start) | async-done | bytes 2097184 | tf_op jit(solution)/shard_map/all_to_all | solution.py:55
  165.6 1.3 copy-done.2
  166.9 4.0 %copy.259 = bf16[2,1,128,8,512]{4,0,3,2,1:T(2,128)(2,1)S(1)} copy(bf16[2,1,128,8,512]{4,3,0,1,2:T(8,128)(2,1)} %bitcast.571) | data formatting | bytes 4194304 | tf_op jit(solution)/shard_map/reshape | solution.py:54
  170.9 10.9 %gather_fusion = bf16[1024,2,512]{2,1,0:T(2,128)(2,1)} fusion(bf16[2,1024,512]{2,0,1:T(2,128)(2,1)S(1)} %bitcast.570, s32[1024]{0:T(1024)S(1)} %fusion.22), kind=kCustom, calls=%fused_computation | custom fusion | bytes 4198400 | tf_op jit(solution)/shard_map/jit(_take)/gather | solution.py:58
  181.8 6.2 %copy.260 = bf16[1024,2,512]{0,2,1:T(8,128)(2,1)} copy(bf16[1024,2,512]{2,1,0:T(2,128)(2,1)} %gather_fusion) | data formatting | bytes 4194304 | tf_op jit(solution)/shard_map/jit(_take)/gather | solution.py:58
  188.0 1.8 bitcast_select_fusion
  189.8 1.1 constant_dynamic-slice_fusion
  190.9 2.6 collective-permute-start
  193.5 3.0 copy.261
  196.5 20.4 %collective-permute-done = bf16[2,1,512,512]{2,3,1,0:T(8,128)(2,1)S(1)} collective-permute-done((bf16[2,1,512,512]{2,3,1,0:T(8,128)(2,1)}, bf16[2,1,512,512]{2,3,1,0:T(8,128)(2,1)S(1)}, u32[]{:S(2)}, u32[]{:S(2)}) %collective-permute-start) | collective-permute-done | bytes 1048608 | tf_op jit(solution)/shard_map/ppermute | solution.py:9
  217.4 2.1 multiply_convert_fusion
  219.5 60.8 %all-gather.2.cloned.1.call-done = bf16[2,1,1024,1024]{3,2,1,0:T(8,128)(2,1)} async-done(((bf16[2,1,1024,512]{3,2,1,0:T(8,128)(2,1)}), bf16[2,1,1024,1024]{3,2,1,0:T(8,128)(2,1)}) %all-gather.2.cloned.1.call-update) | async-done | bytes 4194320 | tf_op jit(solution)/shard_map/all_gather | solution.py:67
  280.3 3.0 fusion.5
  283.3 1.2 fusion.6
  284.5 1.2 add_bitcast_fusion.1
  285.8 1.2 subtract_bitcast_fusion.1
  287.6 1.2 fusion.4
  288.9 1.2 fusion.3
  290.1 1.2 subtract_bitcast_fusion
  291.4 1.3 add_bitcast_fusion
  292.6 2.3 fusion.2
  (111 shorter events, 58.6 us)
Async XLA Ops:
  99.4 15.0 %copy-start.3 = (s32[1024]{0:T(1024)S(1)}, s32[1024]{0:T(1024)}, u32[]{:S(2)}) copy-start(s32[1024]{0:T(1024)} %param.3) | copy-start | bytes 12292
  99.4 66.1 %all-to-all-start = ((bf16[128,2,1,8,512]{4,3,1,2,0:T(8,128)(2,1)}), bf16[128,2,1,8,512]{4,3,1,2,0:T(8,128)(2,1)S(1)}, u32[]{:S(2)}, u32[]{:S(2)}) async-start(bf16[128,2,1,8,512]{4,3,1,2,0:T(8,128)(2,1)} %constant_dynamic-update-slice_fusion), calls=%async_computation | async-start | bytes 4194304 | tf_op jit(solution)/shard_map/all_to_all | solution.py:55
  114.4 165.9 %all-gather.2.cloned.1.call-start = ((), (), s32[]{:S(2)}) async-start(), calls=%async_computation.1 | async-start | bytes 6291456 | tf_op jit(solution)/shard_map/all_gather | solution.py:67
  165.6 1.3 copy-start.2
  190.9 26.0 %collective-permute-start = (bf16[2,1,512,512]{2,3,1,0:T(8,128)(2,1)}, bf16[2,1,512,512]{2,3,1,0:T(8,128)(2,1)S(1)}, u32[]{:S(2)}, u32[]{:S(2)}) collective-permute-start(bf16[2,1,512,512]{2,3,1,0:T(8,128)(2,1)} %constant_dynamic-slice_fusion), channel_id=1, source_target_pairs={{0,1},{1,0},{2,3},{3,2},{4,5},{5,4},{6,7},{7,6},{8,9},{9,8},{10,11... | collective-permute-start | bytes 3145736 | tf_op jit(solution)/shard_map/ppermute | solution.py:9
  196.5 20.9 %copy-start.1 = (f32[2,1,1024,512]{3,2,1,0:T(8,128)S(1)}, f32[2,1,1024,512]{3,2,1,0:T(8,128)}, u32[]{:S(2)}) copy-start(f32[2,1,1024,512]{3,2,1,0:T(8,128)} %copy.261) | copy-start | bytes 12582916
  219.5 60.8 %copy-start = (bf16[2,1,1024,512]{3,2,1,0:T(8,128)(2,1)S(1)}, bf16[2,1,1024,512]{3,2,1,0:T(8,128)(2,1)}, u32[]{:S(2)}) copy-start(bf16[2,1,1024,512]{3,2,1,0:T(8,128)(2,1)} %multiply_convert_fusion) | copy-start | bytes 6291460
  280.3 3.0 copy-start.4
Sparse Core Ops, SparseCore 0:
  219.7 60.5 all-gather.1
